TPU v7x, 128 devices: a whole 4x4x4 slice. The times are simulated.
128 devices in a mesh: row: 8 (over y, core), col: 16 (over z, x).
Axes of the slice: x: 4, y: 4, z: 4, core: 2. Of those that a mesh axis runs over, the one named last changes fastest.
Arguments:
- kernel_panel: float32 [64, 32768], P(None, ('row', 'col')), may hold values from -4 to 16, as said below
- kernel_slab: float32 [32768, 4096], P('row', 'col'), may hold values from -4 to 20, as said below
- targets: float32 [256, 32768], P(None, ('row', 'col')), may hold values from -6 to 6
Outputs:
- updated_slab: float32 [32768, 4096], P('row', 'col')
- solved_targets: float32 [256, 32768], P('col', 'row')
- panel_factor: float32 [64, 32768], P(None, ('row', 'col'))
Inputs may be any that keep to these rules, and one draw needn't show every extreme that they name: kernel_panel[:, 0:64] is symmetric and positive definite. `kernel_slab`: rows 0 to 63 equal kernel_panel[:, 32768 - 4096 : 32768]; the last 4096 rows form a symmetric matrix.
All inputs are finite; a program needn't handle non-finite values.
Results may differ from a plain program's by a relative error of at most 0.00018.
Values sent between devices are 32-bit elements; how exact they have to be, the bound alone decides.
No kernel may reach another device: no remote copies, remote signals or barrier semaphores. Data moves between devices by JAX's collectives and lax.ppermute only.
A program may use at most 64 MiB of HBM per device.

v0:
```python
import jax
import jax.numpy as jnp
from jax import lax
from jax.sharding import PartitionSpec as P


def spread(block, axis, source):
    block = jnp.where(lax.axis_index(axis) == source, block, jnp.zeros_like(block))
    return lax.psum(block, axis)


def lower_solve(factor, values):
    return jax.scipy.linalg.solve_triangular(factor, values, lower=True)


def body(kernel_panel, kernel_slab, targets):
    highest = lax.Precision.HIGHEST
    panel_width = kernel_panel.shape[0]
    row_count = lax.axis_size("row")
    row_index = lax.axis_index("row")
    flat_index = lax.axis_index(("row", "col"))
    corner_rows = jnp.concatenate([kernel_panel[:, :panel_width], targets[:, :panel_width]], 0)
    shared = spread(corner_rows, ("row", "col"), 0)
    lower_factor = jnp.linalg.cholesky(shared[:panel_width])
    panel_factor = lower_solve(lower_factor, kernel_panel)
    gathered = lax.all_gather(panel_factor, "col", axis=1, tiled=True)
    slab_factor = spread(panel_factor, "row", row_count - 1)
    product = lax.dot_general(
        gathered,
        slab_factor,
        (((0,), (0,)), ((), ())),
        precision=highest,
        preferred_element_type=jnp.float32,
    )
    update = kernel_slab - product
    head_rows = jnp.where(row_index == 0, slab_factor, update[:panel_width])
    updated_slab = jnp.concatenate([head_rows, update[panel_width:]], 0)
    solved_lead = lower_solve(lower_factor, shared[panel_width:].T).T
    result = targets - jnp.dot(
        solved_lead, panel_factor, precision=highest, preferred_element_type=jnp.float32
    )
    head_cols = jnp.where(flat_index == 0, solved_lead, result[:, :panel_width])
    result = jnp.concatenate([head_cols, result[:, panel_width:]], 1)
    solved_targets = lax.all_to_all(result, "col", split_axis=0, concat_axis=1, tiled=True)
    return (updated_slab, solved_targets, panel_factor)


def solution(mesh):
    in_specs = (P(None, ("row", "col")), P("row", "col"), P(None, ("row", "col")))
    out_specs = (P("row", "col"), P("col", "row"), P(None, ("row", "col")))
    return jax.shard_map(body, mesh=mesh, in_specs=in_specs, out_specs=out_specs, check_vma=False)
```

profile of v0, /device:TPU:0, one launch (start us, length us, event | category | flops | bytes accessed | tf_op | source)
XLA Modules:
  0.0 286.8 jit_solution(15664791899250229156)
XLA Ops:
  7.2 0.0 all-reduce.3.cloned.1.call-start
  7.2 0.8 slice.34
  8.0 0.1 copy.22
  8.1 1.1 copy.17
  9.2 0.7 maximum_select_fusion
  9.9 0.0 all-reduce.3.cloned.1.call-update
  9.9 0.0 all-reduce.5.cloned.1.call-start
  10.0 143.3 %all-reduce.3.cloned.1.call-done = f32[320,64]{0,1:T(8,128)} async-done(((f32[320,64]{0,1:T(8,128)}), f32[320,64]{0,1:T(8,128)}) %all-reduce.3.cloned.1.call-update) | async-done | bytes 81936 | tf_op jit(solution)/shard_map/psum | solution.py:9
  153.3 0.8 slice.43
  154.1 0.1 copy.18
  154.1 0.8 fusion.5
  154.9 5.8 %cholesky.18 = f32[64,64]{1,0:T(8,128)S(1)} custom-call(f32[64,64]{1,0:T(8,128)S(1)} %fusion.5), custom_call_target="Cholesky" | custom-call | tf_op jit(solution)/shard_map/jit(cholesky)/cholesky | solution.py:24
  160.8 0.6 compare_reduce_fusion
  161.4 0.7 fusion.1
  162.1 4.9 %custom-call.7 = f32[1,64,64]{1,2,0:T(8,128)S(1)} custom-call(f32[1,64,64]{2,1,0:T(8,128)S(1)} %fusion.1), custom_call_target="InvertDiagBlocksLowerTriangular" | custom-call | tf_op jit(solution)/shard_map/jit(_solve_triangular)/triangular_solve | solution.py:13
  167.0 1.8 broadcast_select_fusion
  168.8 0.0 all-reduce.5.cloned.1.call-update
  168.8 0.0 all-gather.2.cloned.1.call-start
  168.8 0.7 all-gather.2.cloned.1.call-update
  169.5 1.2 fusion
  170.7 1.3 convolution_subtract_fusion.1
  172.0 0.8 copy.20
  172.9 5.6 %all-to-all-start = ((f32[16,16,256]{2,1,0:T(8,128)}), f32[16,16,256]{2,1,0:T(8,128)S(1)}, u32[]{:S(2)}, u32[]{:S(2)}) async-start(f32[16,16,256]{2,1,0:T(8,128)} %bitcast.7), calls=%async_computation | async-start | bytes 524288 | tf_op jit(solution)/shard_map/all_to_all | solution.py:44
  178.5 8.7 %all-to-all-done = f32[16,16,256]{2,1,0:T(8,128)S(1)} async-done(((f32[16,16,256]{2,1,0:T(8,128)}), f32[16,16,256]{2,1,0:T(8,128)S(1)}, u32[]{:S(2)}, u32[]{:S(2)}) %all-to-all-start) | async-done | bytes 262176 | tf_op jit(solution)/shard_map/all_to_all | solution.py:44
  187.2 0.7 copy.23
  187.9 38.0 %all-reduce.5.cloned.1.call-done = f32[64,256]{1,0:T(8,128)} async-done(((f32[64,256]{1,0:T(8,128)}), f32[64,256]{1,0:T(8,128)}) %all-reduce.5.cloned.1.call-update) | async-done | bytes 65552 | tf_op jit(solution)/shard_map/psum | solution.py:9
  225.9 45.2 %all-gather.2.cloned.1.call-done = f32[64,4096]{1,0:T(8,128)} async-done(((f32[64,256]{1,0:T(8,128)}), f32[64,4096]{1,0:T(8,128)}) %all-gather.2.cloned.1.call-update) | async-done | bytes 1048592 | tf_op jit(solution)/shard_map/all_gather | solution.py:26
  271.1 6.0 %convolution_subtract_fusion = f32[4096,256]{1,0:T(8,128)S(1)} fusion(f32[4096,256]{1,0:T(8,128)} %param.6, f32[64,4096]{1,0:T(8,128)} %all-gather.2.cloned.1.call-done, f32[64,256]{1,0:T(8,128)} %all-reduce.5.cloned.1.call-done), kind=kOutput, calls=%fused_computation | convolution fusion | flops 806354944 | bytes 9502720 | tf_op jit(solution)/shard_map/dot_general | solution.py:28
  277.1 0.0 copy-start
  277.1 0.3 slice.45
  277.4 0.6 copy-done
  278.0 2.3 pad_maximum_fusion
  (6 shorter events, 0.1 us)
Async XLA Ops:
  7.2 146.1 %all-reduce.3.cloned.1.call-start = ((), (), s32[]{:S(2)}) async-start(), calls=%async_computation.1 | async-start | bytes 196608 | tf_op jit(solution)/shard_map/psum | solution.py:9
  9.9 216.0 %all-reduce.5.cloned.1.call-start = ((), (), s32[]{:S(2)}) async-start(), calls=%async_computation.2 | async-start | bytes 131072 | tf_op jit(solution)/shard_map/psum | solution.py:9
  168.8 102.3 %all-gather.2.cloned.1.call-start = ((), (), s32[]{:S(2)}) async-start(), calls=%async_computation.3 | async-start | bytes 1114112 | tf_op jit(solution)/shard_map/all_gather | solution.py:26
  172.9 14.3 %all-to-all-start = ((f32[16,16,256]{2,1,0:T(8,128)}), f32[16,16,256]{2,1,0:T(8,128)S(1)}, u32[]{:S(2)}, u32[]{:S(2)}) async-start(f32[16,16,256]{2,1,0:T(8,128)} %bitcast.7), calls=%async_computation | async-start | bytes 524288 | tf_op jit(solution)/shard_map/all_to_all | solution.py:44
  277.1 0.8 copy-start
Sparse Core Ops, SparseCore 0:
  13.3 139.9 all-reduce.2
  168.9 56.9 all-reduce.4
  228.6 42.4 all-gather.1
where the time goes:
time: 287 us
  waiting for transfers between devices  236 us (82%)
  other arithmetic  15.9 us (6%)
  between operations  13.9 us (5%)
  matrix products  10.2 us (4%)
  starting transfers between devices  5.75 us (2%)
  local copies, waits for them, and re-layouts  5.16 us (2%)
    psum x2, waiting for transfers between devices, spread(): return lax.psum(block, axis)  181 us
    all_gather x1, waiting for transfers between devices, body(): gathered = lax.all_gather(panel_factor, 'col', axis=1, tiled=True)  45.2 us
    all_to_all x1, waiting for transfers between devices, body(): lax.all_to_all(result, 'col', split_axis=0, concat_axis=1, tiled=True)  8.69 us
    another operation x3, other arithmetic, body(): lower_factor = jnp.linalg.cholesky(shared[:panel_width])  6.52 us
    dot_general x1, matrix products, body(): lax.dot_general(gathered, slab_factor, (((0,), (0,)), ((), ())), precisio...  6 us
  transfers between devices with their start and end apart: 4, of which 4 were waited for; matrix products, arithmetic and copies ran while one was open for 1% of the time, Pallas kernels for 0%

commit v1 on v0

--- a/solution.py
+++ b/solution.py
@@ -2,6 +2,28 @@
 import jax.numpy as jnp
 from jax import lax
 from jax.sharding import PartitionSpec as P
+
+
+def split_up(x, dim, devices):
+    before, after = (x.shape[:dim], x.shape[dim + 1 :])
+    return jnp.moveaxis(x.reshape(*before, devices, -1, *after), dim, 0)
+
+
+def laid_out(blocks, dim):
+    blocks = jnp.moveaxis(blocks, 0, dim)
+    lengths = blocks.shape
+    return blocks.reshape(*lengths[:dim], lengths[dim] * lengths[dim + 1], *lengths[dim + 2 :])
+
+
+def exchange_in_pairs(array, axis, split_dim, concat_dim):
+    count, here = (lax.axis_size(axis), lax.axis_index(axis))
+    blocks = split_up(array, split_dim, count)
+    gathered = [blocks[here]]
+    for lap in range(1, count):
+        sent = blocks[here ^ lap]
+        gathered.append(lax.ppermute(sent, axis, [(i, i ^ lap) for i in range(count)]))
+    blocks = jnp.stack(gathered)[here ^ jnp.arange(count)]
+    return laid_out(blocks, concat_dim)
 
 
 def spread(block, axis, source):
@@ -41,7 +63,7 @@
     )
     head_cols = jnp.where(flat_index == 0, solved_lead, result[:, :panel_width])
     result = jnp.concatenate([head_cols, result[:, panel_width:]], 1)
-    solved_targets = lax.all_to_all(result, "col", split_axis=0, concat_axis=1, tiled=True)
+    solved_targets = exchange_in_pairs(result, "col", 0, 1)
     return (updated_slab, solved_targets, panel_factor)
 
 

time: 287 us -> 289 us (level)
  starting transfers between devices: 5.75 us -> 20.7 us
  waiting for transfers between devices: 236 us -> 223 us
    ppermute x0 -> x15, waiting for transfers between devices: none -> 47.8 us  [exchange_in_pairs(): lax.ppermute(sent, axis, [(i, i ^ lap) for i in range(count)])]
    psum x2, waiting for transfers between devices: 181 us -> 143 us  [spread(): return lax.psum(block, axis)]
    ppermute x0 -> x15, starting transfers between devices: none -> 20.6 us  [exchange_in_pairs(): lax.ppermute(sent, axis, [(i, i ^ lap) for i in range(count)])]
    all_gather x1, waiting for transfers between devices: 45.2 us -> 32.4 us  [body(): gathered = lax.all_gather(panel_factor, 'col', axis=1, tiled=True)]
    all_to_all x1 -> x0, waiting for transfers between devices: 8.69 us -> none  [body(): lax.all_to_all(result, 'col', split_axis=0, concat_axis=1, tiled=True)]
    all_to_all x1 -> x0, starting transfers between devices: 5.63 us -> none  [body(): lax.all_to_all(result, 'col', split_axis=0, concat_axis=1, tiled=True)]
  transfers between devices with their start and end apart: 4 -> 18, of which waited for: 4 -> 12; matrix products, arithmetic and copies ran while one was open for 1% -> 0% of each run, Pallas kernels for 0% -> 0%
where the time goes in v1:
time: 289 us
  waiting for transfers between devices  223 us (77%)
  starting transfers between devices  20.7 us (7%)
  other arithmetic  15.9 us (6%)
  between operations  14.1 us (5%)
  matrix products  9.37 us (3%)
  local copies, waits for them, and re-layouts  5.15 us (2%)
    psum x2, waiting for transfers between devices, spread(): return lax.psum(block, axis)  143 us
    ppermute x15, waiting for transfers between devices, exchange_in_pairs(): lax.ppermute(sent, axis, [(i, i ^ lap) for i in range(count)])  47.8 us
    all_gather x1, waiting for transfers between devices, body(): gathered = lax.all_gather(panel_factor, 'col', axis=1, tiled=True)  32.4 us
    ppermute x15, starting transfers between devices, exchange_in_pairs(): lax.ppermute(sent, axis, [(i, i ^ lap) for i in range(count)])  20.6 us
    another operation x3, other arithmetic, body(): lower_factor = jnp.linalg.cholesky(shared[:panel_width])  6.52 us
    dot_general x1, matrix products, body(): lax.dot_general(gathered, slab_factor, (((0,), (0,)), ((), ())), precisio...  6 us
  transfers between devices with their start and end apart: 18, of which 12 were waited for; matrix products, arithmetic and copies ran while one was open for 0% of the time, Pallas kernels for 0%

profile of v1, /device:TPU:0, one launch (start us, length us, event | category | flops | bytes accessed | tf_op | source)
XLA Modules:
  0.0 288.6 jit_solution(18054009681356506962)
XLA Ops:
  7.2 0.0 all-reduce.3.cloned.1.call-start
  7.2 0.8 slice.34
  8.0 0.1 copy.22
  8.1 1.1 copy.17
  9.2 0.7 maximum_select_fusion
  9.9 0.0 all-reduce.3.cloned.1.call-update
  9.9 0.0 all-reduce.5.cloned.1.call-start
  10.1 143.2 %all-reduce.3.cloned.1.call-done = f32[320,64]{0,1:T(8,128)} async-done(((f32[320,64]{0,1:T(8,128)}), f32[320,64]{0,1:T(8,128)}) %all-reduce.3.cloned.1.call-update) | async-done | bytes 81936 | tf_op jit(solution)/shard_map/psum | solution.py:31
  153.3 0.8 slice.45
  154.1 0.1 copy.18
  154.1 0.8 fusion.5
  154.9 5.8 %cholesky.18 = f32[64,64]{1,0:T(8,128)S(1)} custom-call(f32[64,64]{1,0:T(8,128)S(1)} %fusion.5), custom_call_target="Cholesky" | custom-call | tf_op jit(solution)/shard_map/jit(cholesky)/cholesky | solution.py:46
  160.8 0.6 compare_reduce_fusion
  161.4 0.7 fusion.1
  162.1 4.9 %custom-call.7 = f32[1,64,64]{1,2,0:T(8,128)S(1)} custom-call(f32[1,64,64]{2,1,0:T(8,128)S(1)} %fusion.1), custom_call_target="InvertDiagBlocksLowerTriangular" | custom-call | tf_op jit(solution)/shard_map/jit(_solve_triangular)/triangular_solve | solution.py:35
  167.0 1.7 broadcast_select_fusion
  168.7 0.0 copy-start
  168.7 1.2 fusion
  169.9 0.4 convolution_subtract_fusion.1
  170.4 0.1 copy.20
  170.6 0.0 all-reduce.5.cloned.1.call-update
  170.6 0.0 all-gather.2.cloned.1.call-start
  170.7 0.1 dynamic-slice_bitcast_fusion
  170.7 2.4 collective-permute-start
  173.1 0.0 copy-done
  173.2 0.0 all-gather.2.cloned.1.call-update
  173.2 2.1 collective-permute-start.14
  175.3 2.6 collective-permute-start.13
  177.9 1.5 collective-permute-start.12
  179.4 2.7 collective-permute-start.11
  182.1 0.0 collective-permute-done
  182.1 1.8 collective-permute-start.1
  184.0 3.4 %collective-permute-done.1 = f32[16,256]{1,0:T(8,128)S(1)} collective-permute-done((f32[16,256]{1,0:T(8,128)S(1)}, f32[16,256]{1,0:T(8,128)S(1)}, u32[]{:S(2)}, u32[]{:S(2)}) %collective-permute-start.1) | collective-permute-done | bytes 16416 | tf_op jit(solution)/shard_map/ppermute | solution.py:24
  187.4 1.9 collective-permute-start.2
  189.3 3.0 %collective-permute-done.2 = f32[16,256]{1,0:T(8,128)S(1)} collective-permute-done((f32[16,256]{1,0:T(8,128)S(1)}, f32[16,256]{1,0:T(8,128)S(1)}, u32[]{:S(2)}, u32[]{:S(2)}) %collective-permute-start.2) | collective-permute-done | bytes 16416 | tf_op jit(solution)/shard_map/ppermute | solution.py:24
  192.3 0.0 collective-permute-start.3
  192.3 3.7 %collective-permute-done.3 = f32[16,256]{1,0:T(8,128)S(1)} collective-permute-done((f32[16,256]{1,0:T(8,128)S(1)}, f32[16,256]{1,0:T(8,128)S(1)}, u32[]{:S(2)}, u32[]{:S(2)}) %collective-permute-start.3) | collective-permute-done | bytes 16416 | tf_op jit(solution)/shard_map/ppermute | solution.py:24
  196.1 0.0 collective-permute-start.4
  196.1 4.6 %collective-permute-done.4 = f32[16,256]{1,0:T(8,128)S(1)} collective-permute-done((f32[16,256]{1,0:T(8,128)S(1)}, f32[16,256]{1,0:T(8,128)S(1)}, u32[]{:S(2)}, u32[]{:S(2)}) %collective-permute-start.4) | collective-permute-done | bytes 16416 | tf_op jit(solution)/shard_map/ppermute | solution.py:24
  200.7 1.3 collective-permute-start.5
  202.1 4.8 %collective-permute-done.5 = f32[16,256]{1,0:T(8,128)S(1)} collective-permute-done((f32[16,256]{1,0:T(8,128)S(1)}, f32[16,256]{1,0:T(8,128)S(1)}, u32[]{:S(2)}, u32[]{:S(2)}) %collective-permute-start.5) | collective-permute-done | bytes 16416 | tf_op jit(solution)/shard_map/ppermute | solution.py:24
  206.9 1.3 collective-permute-start.6
  208.2 4.5 %collective-permute-done.6 = f32[16,256]{1,0:T(8,128)S(1)} collective-permute-done((f32[16,256]{1,0:T(8,128)S(1)}, f32[16,256]{1,0:T(8,128)S(1)}, u32[]{:S(2)}, u32[]{:S(2)}) %collective-permute-start.6) | collective-permute-done | bytes 16416 | tf_op jit(solution)/shard_map/ppermute | solution.py:24
  212.7 0.0 collective-permute-start.7
  212.7 5.2 %collective-permute-done.7 = f32[16,256]{1,0:T(8,128)S(1)} collective-permute-done((f32[16,256]{1,0:T(8,128)S(1)}, f32[16,256]{1,0:T(8,128)S(1)}, u32[]{:S(2)}, u32[]{:S(2)}) %collective-permute-start.7) | collective-permute-done | bytes 16416 | tf_op jit(solution)/shard_map/ppermute | solution.py:24
  218.0 0.0 collective-permute-start.8
  218.0 6.1 %collective-permute-done.8 = f32[16,256]{1,0:T(8,128)S(1)} collective-permute-done((f32[16,256]{1,0:T(8,128)S(1)}, f32[16,256]{1,0:T(8,128)S(1)}, u32[]{:S(2)}, u32[]{:S(2)}) %collective-permute-start.8) | collective-permute-done | bytes 16416 | tf_op jit(solution)/shard_map/ppermute | solution.py:24
  224.1 1.3 collective-permute-start.9
  225.4 6.3 %collective-permute-done.9 = f32[16,256]{1,0:T(8,128)S(1)} collective-permute-done((f32[16,256]{1,0:T(8,128)S(1)}, f32[16,256]{1,0:T(8,128)S(1)}, u32[]{:S(2)}, u32[]{:S(2)}) %collective-permute-start.9) | collective-permute-done | bytes 16416 | tf_op jit(solution)/shard_map/ppermute | solution.py:24
  231.8 1.5 collective-permute-start.10
  233.2 5.9 %collective-permute-done.10 = f32[16,256]{1,0:T(8,128)S(1)} collective-permute-done((f32[16,256]{1,0:T(8,128)S(1)}, f32[16,256]{1,0:T(8,128)S(1)}, u32[]{:S(2)}, u32[]{:S(2)}) %collective-permute-start.10) | collective-permute-done | bytes 16416 | tf_op jit(solution)/shard_map/ppermute | solution.py:24
  239.1 0.0 collective-permute-done.11
  239.1 0.0 collective-permute-done.12
  239.2 0.0 collective-permute-done.13
  239.2 0.0 collective-permute-done.14
  239.2 0.6 gather_fusion
  239.8 0.7 copy.23
  240.5 0.0 all-reduce.5.cloned.1.call-done
  240.5 32.4 %all-gather.2.cloned.1.call-done = f32[64,4096]{1,0:T(8,128)} async-done(((f32[64,256]{1,0:T(8,128)}), f32[64,4096]{1,0:T(8,128)}) %all-gather.2.cloned.1.call-update) | async-done | bytes 1048592 | tf_op jit(solution)/shard_map/all_gather | solution.py:48
  272.9 6.0 %convolution_subtract_fusion = f32[4096,256]{1,0:T(8,128)S(1)} fusion(f32[4096,256]{1,0:T(8,128)} %param.6, f32[64,4096]{1,0:T(8,128)} %all-gather.2.cloned.1.call-done, f32[64,256]{1,0:T(8,128)} %all-reduce.5.cloned.1.call-done), kind=kOutput, calls=%fused_computation.1 | convolution fusion | flops 806354944 | bytes 9502720 | tf_op jit(solution)/shard_map/dot_general | solution.py:50
  278.9 0.0 copy-start.1
  278.9 0.3 slice.47
  279.2 0.6 copy-done.1
  279.7 2.3 pad_maximum_fusion
  (23 shorter events, 0.1 us)
Async XLA Ops:
  7.2 146.1 %all-reduce.3.cloned.1.call-start = ((), (), s32[]{:S(2)}) async-start(), calls=%async_computation | async-start | bytes 196608 | tf_op jit(solution)/shard_map/psum | solution.py:31
  9.9 230.6 %all-reduce.5.cloned.1.call-start = ((), (), s32[]{:S(2)}) async-start(), calls=%async_computation.1 | async-start | bytes 131072 | tf_op jit(solution)/shard_map/psum | solution.py:31
  168.7 4.4 %copy-start = (f32[64,256]{1,0:T(8,128)}, f32[64,256]{1,0:T(8,128)S(1)}, u32[]{:S(2)}) copy-start(f32[64,256]{1,0:T(8,128)S(1)} %get-tuple-element.21) | copy-start | bytes 196612
  170.6 102.3 %all-gather.2.cloned.1.call-start = ((), (), s32[]{:S(2)}) async-start(), calls=%async_computation.2 | async-start | bytes 1114112 | tf_op jit(solution)/shard_map/all_gather | solution.py:48
  170.7 11.4 %collective-permute-start = (f32[16,256]{1,0:T(8,128)S(1)}, f32[16,256]{1,0:T(8,128)S(1)}, u32[]{:S(2)}, u32[]{:S(2)}) collective-permute-start(f32[16,256]{1,0:T(8,128)S(1)} %get-tuple-element.18), channel_id=1, source_target_pairs={{0,1},{1,0},{2,3},{3,2},{4,5},{5,4},{6,7},{7,6},{8,9},{9,8},{10,11... | collective-permute-start | bytes 49160 | tf_op jit(solution)/shard_map/ppermute | solution.py:24
  173.2 66.0 %collective-permute-start.14 = (f32[16,256]{1,0:T(8,128)S(1)}, f32[16,256]{1,0:T(8,128)S(1)}, u32[]{:S(2)}, u32[]{:S(2)}) collective-permute-start(f32[16,256]{1,0:T(8,128)S(1)} %get-tuple-element.4), channel_id=1, source_target_pairs={{0,15},{1,14},{2,13},{3,12},{4,11},{5,10},{6,9},{7,8},{8,7},{9,6},... | collective-permute-start | bytes 49160 | tf_op jit(solution)/shard_map/ppermute | solution.py:24
  175.3 63.8 %collective-permute-start.13 = (f32[16,256]{1,0:T(8,128)S(1)}, f32[16,256]{1,0:T(8,128)S(1)}, u32[]{:S(2)}, u32[]{:S(2)}) collective-permute-start(f32[16,256]{1,0:T(8,128)S(1)} %get-tuple-element.5), channel_id=1, source_target_pairs={{0,14},{1,15},{2,12},{3,13},{4,10},{5,11},{6,8},{7,9},{8,6},{9,7},... | collective-permute-start | bytes 49160 | tf_op jit(solution)/shard_map/ppermute | solution.py:24
  177.9 61.2 %collective-permute-start.12 = (f32[16,256]{1,0:T(8,128)S(1)}, f32[16,256]{1,0:T(8,128)S(1)}, u32[]{:S(2)}, u32[]{:S(2)}) collective-permute-start(f32[16,256]{1,0:T(8,128)S(1)} %get-tuple-element.6), channel_id=1, source_target_pairs={{0,13},{1,12},{2,15},{3,14},{4,9},{5,8},{6,11},{7,10},{8,5},{9,4},... | collective-permute-start | bytes 49160 | tf_op jit(solution)/shard_map/ppermute | solution.py:24
  179.4 59.7 %collective-permute-start.11 = (f32[16,256]{1,0:T(8,128)S(1)}, f32[16,256]{1,0:T(8,128)S(1)}, u32[]{:S(2)}, u32[]{:S(2)}) collective-permute-start(f32[16,256]{1,0:T(8,128)S(1)} %get-tuple-element.7), channel_id=1, source_target_pairs={{0,12},{1,13},{2,14},{3,15},{4,8},{5,9},{6,10},{7,11},{8,4},{9,5},... | collective-permute-start | bytes 49160 | tf_op jit(solution)/shard_map/ppermute | solution.py:24
  182.1 5.2 %collective-permute-start.1 = (f32[16,256]{1,0:T(8,128)S(1)}, f32[16,256]{1,0:T(8,128)S(1)}, u32[]{:S(2)}, u32[]{:S(2)}) collective-permute-start(f32[16,256]{1,0:T(8,128)S(1)} %get-tuple-element.17), channel_id=1, source_target_pairs={{0,2},{1,3},{2,0},{3,1},{4,6},{5,7},{6,4},{7,5},{8,10},{9,11},{10,... | collective-permute-start | bytes 49160 | tf_op jit(solution)/shard_map/ppermute | solution.py:24
  187.4 4.9 %collective-permute-start.2 = (f32[16,256]{1,0:T(8,128)S(1)}, f32[16,256]{1,0:T(8,128)S(1)}, u32[]{:S(2)}, u32[]{:S(2)}) collective-permute-start(f32[16,256]{1,0:T(8,128)S(1)} %get-tuple-element.16), channel_id=1, source_target_pairs={{0,3},{1,2},{2,1},{3,0},{4,7},{5,6},{6,5},{7,4},{8,11},{9,10},{10,... | collective-permute-start | bytes 49160 | tf_op jit(solution)/shard_map/ppermute | solution.py:24
  192.3 3.7 %collective-permute-start.3 = (f32[16,256]{1,0:T(8,128)S(1)}, f32[16,256]{1,0:T(8,128)S(1)}, u32[]{:S(2)}, u32[]{:S(2)}) collective-permute-start(f32[16,256]{1,0:T(8,128)S(1)} %get-tuple-element.15), channel_id=1, source_target_pairs={{0,4},{1,5},{2,6},{3,7},{4,0},{5,1},{6,2},{7,3},{8,12},{9,13},{10,... | collective-permute-start | bytes 49160 | tf_op jit(solution)/shard_map/ppermute | solution.py:24
  196.1 4.6 %collective-permute-start.4 = (f32[16,256]{1,0:T(8,128)S(1)}, f32[16,256]{1,0:T(8,128)S(1)}, u32[]{:S(2)}, u32[]{:S(2)}) collective-permute-start(f32[16,256]{1,0:T(8,128)S(1)} %get-tuple-element.14), channel_id=1, source_target_pairs={{0,5},{1,4},{2,7},{3,6},{4,1},{5,0},{6,3},{7,2},{8,13},{9,12},{10,... | collective-permute-start | bytes 49160 | tf_op jit(solution)/shard_map/ppermute | solution.py:24
  200.7 6.1 %collective-permute-start.5 = (f32[16,256]{1,0:T(8,128)S(1)}, f32[16,256]{1,0:T(8,128)S(1)}, u32[]{:S(2)}, u32[]{:S(2)}) collective-permute-start(f32[16,256]{1,0:T(8,128)S(1)} %get-tuple-element.13), channel_id=1, source_target_pairs={{0,6},{1,7},{2,4},{3,5},{4,2},{5,3},{6,0},{7,1},{8,14},{9,15},{10,... | collective-permute-start | bytes 49160 | tf_op jit(solution)/shard_map/ppermute | solution.py:24
  206.9 5.9 %collective-permute-start.6 = (f32[16,256]{1,0:T(8,128)S(1)}, f32[16,256]{1,0:T(8,128)S(1)}, u32[]{:S(2)}, u32[]{:S(2)}) collective-permute-start(f32[16,256]{1,0:T(8,128)S(1)} %get-tuple-element.12), channel_id=1, source_target_pairs={{0,7},{1,6},{2,5},{3,4},{4,3},{5,2},{6,1},{7,0},{8,15},{9,14},{10,... | collective-permute-start | bytes 49160 | tf_op jit(solution)/shard_map/ppermute | solution.py:24
  212.7 5.2 %collective-permute-start.7 = (f32[16,256]{1,0:T(8,128)S(1)}, f32[16,256]{1,0:T(8,128)S(1)}, u32[]{:S(2)}, u32[]{:S(2)}) collective-permute-start(f32[16,256]{1,0:T(8,128)S(1)} %get-tuple-element.11), channel_id=1, source_target_pairs={{0,8},{1,9},{2,10},{3,11},{4,12},{5,13},{6,14},{7,15},{8,0},{9,1},... | collective-permute-start | bytes 49160 | tf_op jit(solution)/shard_map/ppermute | solution.py:24
  218.0 6.1 %collective-permute-start.8 = (f32[16,256]{1,0:T(8,128)S(1)}, f32[16,256]{1,0:T(8,128)S(1)}, u32[]{:S(2)}, u32[]{:S(2)}) collective-permute-start(f32[16,256]{1,0:T(8,128)S(1)} %get-tuple-element.10), channel_id=1, source_target_pairs={{0,9},{1,8},{2,11},{3,10},{4,13},{5,12},{6,15},{7,14},{8,1},{9,0},... | collective-permute-start | bytes 49160 | tf_op jit(solution)/shard_map/ppermute | solution.py:24
  224.1 7.6 %collective-permute-start.9 = (f32[16,256]{1,0:T(8,128)S(1)}, f32[16,256]{1,0:T(8,128)S(1)}, u32[]{:S(2)}, u32[]{:S(2)}) collective-permute-start(f32[16,256]{1,0:T(8,128)S(1)} %get-tuple-element.9), channel_id=1, source_target_pairs={{0,10},{1,11},{2,8},{3,9},{4,14},{5,15},{6,12},{7,13},{8,2},{9,3},... | collective-permute-start | bytes 49160 | tf_op jit(solution)/shard_map/ppermute | solution.py:24
  231.8 7.4 %collective-permute-start.10 = (f32[16,256]{1,0:T(8,128)S(1)}, f32[16,256]{1,0:T(8,128)S(1)}, u32[]{:S(2)}, u32[]{:S(2)}) collective-permute-start(f32[16,256]{1,0:T(8,128)S(1)} %get-tuple-element.8), channel_id=1, source_target_pairs={{0,11},{1,10},{2,9},{3,8},{4,15},{5,14},{6,13},{7,12},{8,3},{9,2},... | collective-permute-start | bytes 49160 | tf_op jit(solution)/shard_map/ppermute | solution.py:24
  278.9 0.8 copy-start.1
Sparse Core Ops, SparseCore 0:
  13.3 139.9 all-reduce.2
  170.7 56.8 all-reduce.4
  230.3 42.5 all-gather.1
